TPU v7x, 32 devices: a whole 2x2x4 slice. The times are simulated.
32 devices in a mesh: img: 4 (over z), sy: 2 (over x), sx: 4 (over y, core).
Axes of the slice: x: 2, y: 2, z: 4, core: 2. Of those that a mesh axis runs over, the one named last changes fastest.
Arguments:
- memory: bfloat16 [8, 20480, 256], P('img', ('sy', 'sx')), may hold values from -6 to 6
- enc_weight: bfloat16 [256, 256], replicated, may hold values from -0.375 to 0.375
- enc_bias: float32 [256], replicated, may hold values from -4 to 4
- norm_gain: float32 [256], replicated, may hold values from 0.25 to 1.75
- norm_bias: float32 [256], replicated, may hold values from -3 to 3
- class_weight: bfloat16 [256, 91], replicated, may hold values from -0.375 to 0.375
- class_bias: float32 [91], replicated, may hold values from -4 to 4
- box_w1: bfloat16 [256, 256], replicated, may hold values from -0.375 to 0.375
- box_b1: float32 [256], replicated, may hold values from -3 to 3
- box_w2: bfloat16 [256, 256], replicated, may hold values from -0.375 to 0.375
- box_b2: float32 [256], replicated, may hold values from -3 to 3
- box_w3: bfloat16 [256, 4], replicated, may hold values from -0.375 to 0.375
- box_b3: float32 [4], replicated, may hold values from -3 to 3
- picked: int32 [8, 320], P('img', ('sy', 'sx')), may hold values from 0 to 2559, as said below
- counts: int32 [8, 8], P('img', ('sy', 'sx')), may hold values from 1 to 40, 80 in all within a row
Outputs:
- token_logits: bfloat16 [8, 91, 20480], P('img', None, ('sy', 'sx'))
- token_boxes: float32 [8, 4, 20480], P('img', None, ('sy', 'sx'))
- query_feat: bfloat16 [8, 80, 256], P(None, 'img')
- query_logits: bfloat16 [8, 80, 91], P(None, 'img')
- query_boxes: bfloat16 [8, 80, 4], P(None, 'img')
Inputs may be any that keep to these rules, and one draw needn't show every extreme that they name: `picked`: each tile's 40 entries are distinct local token indices in rising order; only the first counts of them are selected. Each image's counts sum to 80.
All inputs are finite; a program needn't handle non-finite values. No bound on the sum of `counts` on one device may be relied on, other than what follows from the above.
Results may differ from a plain program's by a relative error of at most 0.0041.
Values may be sent and summed in bfloat16 or wider, within the bound.
A program may use at most 64 MiB of HBM per device.

v0:
```python
import jax
import jax.numpy as jnp
from jax import lax
from jax.sharding import PartitionSpec as P

TILE_H = 40
TILE_W = 64
Q_DEV = 20


def place_rows(slot, valid, queries, feats, logits, boxes):
    slot_ids = jnp.arange(queries)
    placed = (slot[:, None, :] == slot_ids[None, :, None]) & valid[:, None, :]
    placed_bf = placed.astype(jnp.bfloat16)
    feat_part = jnp.einsum("iqm,imd->iqd", placed_bf, feats, preferred_element_type=jnp.float32)
    logit_part = jnp.einsum("iqm,imc->iqc", placed_bf, logits, preferred_element_type=jnp.float32)
    box_part = jnp.einsum("iqm,imk->iqk", placed_bf, boxes, preferred_element_type=jnp.float32)
    return (feat_part, logit_part, box_part)


def shards(
    memory,
    enc_weight,
    enc_bias,
    norm_gain,
    norm_bias,
    class_weight,
    class_bias,
    box_w1,
    box_b1,
    box_w2,
    box_b2,
    box_w3,
    box_b3,
    picked,
    counts,
):
    images, tok_dev, width = memory.shape
    most = picked.shape[1]
    queries = Q_DEV * lax.axis_size("img")
    shard = lax.axis_index(("sy", "sx"))
    cols_axis = lax.axis_size("sx")
    map_h = TILE_H * lax.axis_size("sy")
    map_w = TILE_W * cols_axis
    flat = memory.reshape(images * tok_dev, width)
    pre = jnp.dot(flat, enc_weight, preferred_element_type=jnp.float32) + enc_bias
    mean = jnp.mean(pre, axis=-1, keepdims=True)
    centered = pre - mean
    var = jnp.mean(centered * centered, axis=-1, keepdims=True)
    out_mem = (centered * lax.rsqrt(var + 1e-05) * norm_gain + norm_bias).astype(jnp.bfloat16)
    hidden = jax.nn.relu(
        jnp.dot(out_mem, box_w1, preferred_element_type=jnp.float32) + box_b1
    ).astype(jnp.bfloat16)
    hidden = jax.nn.relu(
        jnp.dot(hidden, box_w2, preferred_element_type=jnp.float32) + box_b2
    ).astype(jnp.bfloat16)
    mem_three = out_mem.reshape(images, tok_dev, width)
    token_logits = (
        jnp.einsum("dc,itd->ict", class_weight, mem_three, preferred_element_type=jnp.float32)
        + class_bias[None, :, None]
    ).astype(jnp.bfloat16)
    delta = (
        jnp.einsum(
            "dk,itd->ikt",
            box_w3,
            hidden.reshape(images, tok_dev, width),
            preferred_element_type=jnp.float32,
        )
        + box_b3[None, :, None]
    )
    local = jnp.arange(tok_dev)
    row = shard // cols_axis * TILE_H + local // TILE_W
    col = shard % cols_axis * TILE_W + local % TILE_W
    center_x = (col.astype(jnp.float32) + 0.5) / map_w
    center_y = (row.astype(jnp.float32) + 0.5) / map_h
    sizes_wh = jnp.full((tok_dev,), 0.05, jnp.float32)
    prior = jnp.stack([center_x, center_y, sizes_wh, sizes_wh])
    token_boxes = jax.nn.sigmoid(delta + jnp.log(prior / (1.0 - prior))[None])
    sel_feat = jnp.take_along_axis(mem_three, picked[:, :, None], axis=1)
    sel_logits = jnp.transpose(
        jnp.take_along_axis(token_logits, picked[:, None, :], axis=2), (0, 2, 1)
    )
    sel_boxes = jnp.transpose(
        jnp.take_along_axis(token_boxes, picked[:, None, :], axis=2), (0, 2, 1)
    ).astype(jnp.bfloat16)
    steps = jnp.arange(most)
    full_counts = lax.all_gather(counts, ("sy", "sx"), axis=1, tiled=True)
    feats, logits, boxes = (
        lax.all_gather(sel_feat, ("sy", "sx"), axis=1, tiled=True),
        lax.all_gather(sel_logits, ("sy", "sx"), axis=1, tiled=True),
        lax.all_gather(sel_boxes, ("sy", "sx"), axis=1, tiled=True),
    )
    starts = jnp.cumsum(full_counts, axis=1) - full_counts
    slot = (starts[:, :, None] + steps[None, None, :]).reshape(images, -1)
    valid = (steps[None, None, :] < full_counts[:, :, None]).reshape(images, -1)
    feat_all, logit_all, box_all = place_rows(slot, valid, queries, feats, logits, boxes)
    gathered = (
        feat_all.astype(jnp.bfloat16),
        logit_all.astype(jnp.bfloat16),
        box_all.astype(jnp.bfloat16),
    )
    query_feat, query_logits, query_boxes = (
        lax.all_to_all(gathered[0], "img", split_axis=1, concat_axis=0, tiled=True),
        lax.all_to_all(gathered[1], "img", split_axis=1, concat_axis=0, tiled=True),
        lax.all_to_all(gathered[2], "img", split_axis=1, concat_axis=0, tiled=True),
    )
    return (token_logits, token_boxes, query_feat, query_logits, query_boxes)


def solution(mesh):
    return jax.shard_map(
        shards,
        mesh=mesh,
        in_specs=(
            P("img", ("sy", "sx"), None),
            P(),
            P(),
            P(),
            P(),
            P(),
            P(),
            P(),
            P(),
            P(),
            P(),
            P(),
            P(),
            P("img", ("sy", "sx")),
            P("img", ("sy", "sx")),
        ),
        out_specs=(
            P("img", None, ("sy", "sx")),
            P("img", None, ("sy", "sx")),
            P(None, "img", None),
            P(None, "img", None),
            P(None, "img", None),
        ),
        check_vma=False,
    )
```

profile of v0, /device:TPU:0, one launch (start us, length us, event | category | flops | bytes accessed | tf_op | source)
XLA Modules:
  0.0 106.1 jit_solution(10533029599666838307)
XLA Ops:
  0.7 0.8 bitcast_or_fusion
  2.4 1.9 %fusion.35 = (f32[5120]{0:T(1024)S(1)}, f32[5120,256]{1,0:T(8,128)S(1)}) fusion(f32[256]{0:T(256)} %param.17, bf16[5120,256]{1,0:T(8,128)(2,1)S(1)} %bitcast.57, bf16[256,256]{1,0:T(8,128)(2,1)} %param.16), kind=kOutput, calls=%fused_computation.63 | convolution fusion | flops 673704960 | bytes 8016896 | tf_op jit(solution)/shard_map/dot_general | solution.py:46
  4.3 3.0 %multiply_reduce_fusion = f32[5120]{0:T(1024)S(1)} fusion(f32[5120,256]{1,0:T(8,128)S(1)} %get-tuple-element.26, f32[5120]{0:T(1024)S(1)} %broadcast_multiply_fusion), kind=kLoop, calls=%fused_computation.11 | loop fusion | flops 3927040 | bytes 5283840 | tf_op jit(solution)/shard_map/reduce_sum | solution.py:49
  7.5 10.3 %all-gather = s32[8,1,2]{2,1,0:T(1,128)S(1)} all-gather(s32[1,1,2]{2,1,0:T(1,128)S(1)} %bitcast.71), channel_id=1, replica_groups=mesh['img'=4,'sy'=2,'sx'=4] {'sy','sx'}, dimensions={0}, use_global_device_ids=true | all-gather | bytes 72 | tf_op jit(solution)/shard_map/all_gather | solution.py:87
  18.6 6.1 %add_convert_fusion = bf16[5120,256]{1,0:T(8,128)(2,1)} fusion(f32[5120,256]{1,0:T(8,128)} %copy-done.1, f32[256]{0:T(256)S(1)} %copy-done.6, f32[256]{0:T(256)S(1)} %copy-done.7, f32[5120]{0:T(1024)S(1)} %add_rsqrt_fusion, f32[5120]{0:T(1024)S(1)} %broadcast_multiply_fusion), kind=kLoop, calls=%fused_computation.10 | loop fusion | flops 6553600 | bytes 7907328 | tf_op jit(solution)/shard_map/convert_element_type | solution.py:50
  24.9 4.9 %fusion.2 = bf16[5120,256]{1,0:T(8,128)(2,1)} fusion(bf16[256,256]{1,0:T(8,128)(2,1)S(1)} %copy-done.10, f32[256]{0:T(256)S(1)} %copy-done.12, bf16[5120,256]{1,0:T(8,128)(2,1)} %add_convert_fusion, bf16[256,256]{1,0:T(8,128)(2,1)S(1)} %copy-done.11, f32[256]{0:T(256)S(1)} %copy-done.13), kind=kOutput, calls=%fused_computation.8 | convolution fusion | flops 1350041600 | bytes 5507072 | tf_op jit(solution)/shard_map/dot_general | solution.py:55
  29.8 2.6 %fusion.11 = f32[2,4,2560]{2,1,0:T(4,128)S(1)} fusion(bf16[2,2560,256]{2,1,0:T(8,128)(2,1)} %bitcast.60, f32[4,2560]{1,0:T(4,128)S(1)} %fusion.24, f32[4]{0:T(128)S(1)} %copy-done.9, bf16[256,4]{0,1:T(4,128)(2,1)S(1)} %copy-done.4), kind=kOutput, calls=%fused_computation.21 | convolution fusion | flops 10588160 | bytes 2746384 | tf_op jit(solution)/shard_map/dk,itd->ikt/dot_general | solution.py:63
  32.4 1.6 %copy.53 = bf16[2,4,2560]{1,2,0:T(8,128)(2,1)} copy(f32[2,4,2560]{2,1,0:T(4,128)S(1)} %fusion.11) | data formatting | bytes 122880 | tf_op jit(solution)/shard_map/div | solution.py:78
  33.9 3.8 %gather_fusion.2 = bf16[80,4]{1,0:T(8,128)(2,1)S(1)} fusion(bf16[2,4,2560]{1,2,0:T(8,128)(2,1)} %copy.53, s32[80]{0:T(128)S(1)} %reshape.203), kind=kCustom, calls=%fused_computation.2 | custom fusion | bytes 1920 | tf_op jit(solution)/shard_map/jit(take_along_axis)/gather | solution.py:84
  37.9 9.2 %all_gather.15 = bf16[2,320,4]{2,0,1:T(2,128)(2,1)S(1)} all-gather(bf16[2,40,4]{2,0,1:T(2,128)(2,1)S(1)} %copy.55), channel_id=1, replica_groups=mesh['img'=4,'sy'=2,'sx'=4] {'sy','sx'}, dimensions={1}, use_global_device_ids=true | all-gather | bytes 5760 | tf_op jit(solution)/shard_map/all_gather | solution.py:91
  47.4 0.8 copy.57
  48.1 4.9 %all-to-all-start.2 = ((bf16[2,80,4]{2,0,1:T(2,128)(2,1)}), bf16[2,80,4]{2,0,1:T(2,128)(2,1)S(1)}, u32[]{:S(2)}, u32[]{:S(2)}) async-start(bf16[2,80,4]{2,0,1:T(2,128)(2,1)} %copy.57), calls=%async_computation.2 | async-start | bytes 81920 | tf_op jit(solution)/shard_map/all_to_all | solution.py:105
  53.0 3.6 %gather_fusion = bf16[80,256]{1,0:T(8,128)(2,1)S(1)} fusion(bf16[2,2560,256]{2,1,0:T(8,128)(2,1)} %bitcast.58, s32[80]{0:T(128)S(1)} %reshape.203), kind=kCustom, calls=%fused_computation | custom fusion | bytes 82560 | tf_op jit(solution)/shard_map/jit(take_along_axis)/gather | solution.py:79
  56.7 3.6 %fusion.5 = bf16[2,91,2560]{2,1,0:T(8,128)(2,1)} fusion(bf16[2,2560,256]{2,1,0:T(8,128)(2,1)} %bitcast.59, f32[91]{0:T(128)S(1)} %copy-done.5, bf16[256,91]{0,1:T(8,128)(2,1)S(1)} %copy-done.3), kind=kOutput, calls=%fused_computation.14 | convolution fusion | flops 239482880 | bytes 3600236 | tf_op jit(solution)/shard_map/dc,itd->ict/dot_general | solution.py:59
  60.3 2.5 %copy.50 = bf16[2,91,2560]{1,2,0:T(8,128)(2,1)} copy(bf16[2,91,2560]{2,1,0:T(8,128)(2,1)} %fusion.5) | data formatting | bytes 1863680 | tf_op jit(solution)/shard_map/convert_element_type | solution.py:61
  62.8 3.8 %gather_fusion.1 = bf16[80,91]{1,0:T(8,128)(2,1)S(1)} fusion(bf16[2,91,2560]{1,2,0:T(8,128)(2,1)} %copy.50, s32[80]{0:T(128)S(1)} %reshape.203), kind=kCustom, calls=%fused_computation.1 | custom fusion | bytes 29760 | tf_op jit(solution)/shard_map/jit(take_along_axis)/gather | solution.py:81
  66.6 8.5 %all_gather.14 = bf16[2,320,91]{2,1,0:T(8,128)(2,1)S(1)} all-gather(bf16[2,40,91]{2,1,0:T(8,128)(2,1)S(1)} %broadcast_select_fusion.1), channel_id=1, replica_groups=mesh['img'=4,'sy'=2,'sx'=4] {'sy','sx'}, dimensions={1}, use_global_device_ids=true | all-gather | bytes 131040 | tf_op jit(solution)/shard_map/all_gather | solution.py:90
  75.3 9.5 %all_gather.13 = bf16[2,320,256]{2,1,0:T(8,128)(2,1)S(1)} all-gather(bf16[2,40,256]{2,1,0:T(8,128)(2,1)S(1)} %broadcast_select_fusion), channel_id=1, replica_groups=mesh['img'=4,'sy'=2,'sx'=4] {'sy','sx'}, dimensions={1}, use_global_device_ids=true | all-gather | bytes 368640 | tf_op jit(solution)/shard_map/all_gather | solution.py:89
  85.5 5.1 %all-to-all-start.1 = ((bf16[2,80,91]{2,0,1:T(2,128)(2,1)}), bf16[2,80,91]{2,0,1:T(2,128)(2,1)S(1)}, u32[]{:S(2)}, u32[]{:S(2)}) async-start(bf16[2,80,91]{2,0,1:T(2,128)(2,1)} %copy.51), calls=%async_computation.1 | async-start | bytes 81920 | tf_op jit(solution)/shard_map/all_to_all | solution.py:104
  91.5 4.8 %all-to-all-done.1 = bf16[2,80,91]{2,0,1:T(2,128)(2,1)S(1)} async-done(((bf16[2,80,91]{2,0,1:T(2,128)(2,1)}), bf16[2,80,91]{2,0,1:T(2,128)(2,1)S(1)}, u32[]{:S(2)}, u32[]{:S(2)}) %all-to-all-start.1) | async-done | bytes 29152 | tf_op jit(solution)/shard_map/all_to_all | solution.py:104
  96.3 3.3 %all-to-all-start = ((bf16[2,80,256]{2,0,1:T(2,128)(2,1)}), bf16[2,80,256]{2,0,1:T(2,128)(2,1)S(1)}, u32[]{:S(2)}, u32[]{:S(2)}) async-start(bf16[2,80,256]{2,0,1:T(2,128)(2,1)} %copy.48), calls=%async_computation | async-start | bytes 163840 | tf_op jit(solution)/shard_map/all_to_all | solution.py:103
  99.6 3.1 %copy.59 = bf16[2,91,2560]{2,0,1:T(2,128)(2,1)} copy(bf16[2,91,2560]{2,1,0:T(8,128)(2,1)} %fusion.5) | data formatting | bytes 1863680
  102.7 0.7 copy.58
  104.1 1.3 %all-to-all-done = bf16[2,80,256]{2,0,1:T(2,128)(2,1)S(1)} async-done(((bf16[2,80,256]{2,0,1:T(2,128)(2,1)}), bf16[2,80,256]{2,0,1:T(2,128)(2,1)S(1)}, u32[]{:S(2)}, u32[]{:S(2)}) %all-to-all-start) | async-done | bytes 81952 | tf_op jit(solution)/shard_map/all_to_all | solution.py:103
  (61 shorter events, 5.6 us)
Async XLA Ops:
  0.6 1.8 %copy-start = (bf16[2,2560,256]{2,1,0:T(8,128)(2,1)S(1)}, bf16[2,2560,256]{2,1,0:T(8,128)(2,1)}, u32[]{:S(2)}) copy-start(bf16[2,2560,256]{2,1,0:T(8,128)(2,1)} %param.15) | copy-start | bytes 7864324
  4.3 3.1 %copy-start.1 = (f32[5120,256]{1,0:T(8,128)}, f32[5120,256]{1,0:T(8,128)S(1)}, u32[]{:S(2)}) copy-start(f32[5120,256]{1,0:T(8,128)S(1)} %get-tuple-element.26) | copy-start | bytes 15728644
  4.3 3.2 %copy-start.8 = (s32[2,1]{0,1:T(1,128)S(1)}, s32[2,1]{0,1:T(1,128)}, u32[]{:S(2)}) copy-start(s32[2,1]{0,1:T(1,128)} %param.29) | copy-start | bytes 28
  4.3 14.3 %copy-start.6 = (f32[256]{0:T(256)S(1)}, f32[256]{0:T(256)}, u32[]{:S(2)}) copy-start(f32[256]{0:T(256)} %param.19) | copy-start | bytes 3076
  4.3 14.3 %copy-start.7 = (f32[256]{0:T(256)S(1)}, f32[256]{0:T(256)}, u32[]{:S(2)}) copy-start(f32[256]{0:T(256)} %param.18) | copy-start | bytes 3076
  18.6 6.2 %copy-start.10 = (bf16[256,256]{1,0:T(8,128)(2,1)S(1)}, bf16[256,256]{1,0:T(8,128)(2,1)}, u32[]{:S(2)}) copy-start(bf16[256,256]{1,0:T(8,128)(2,1)} %param.24) | copy-start | bytes 393220
  18.6 6.2 %copy-start.11 = (bf16[256,256]{1,0:T(8,128)(2,1)S(1)}, bf16[256,256]{1,0:T(8,128)(2,1)}, u32[]{:S(2)}) copy-start(bf16[256,256]{1,0:T(8,128)(2,1)} %param.22) | copy-start | bytes 393220
  18.6 6.2 %copy-start.12 = (f32[256]{0:T(256)S(1)}, f32[256]{0:T(256)}, u32[]{:S(2)}) copy-start(f32[256]{0:T(256)} %param.25) | copy-start | bytes 3076
  18.6 6.2 %copy-start.13 = (f32[256]{0:T(256)S(1)}, f32[256]{0:T(256)}, u32[]{:S(2)}) copy-start(f32[256]{0:T(256)} %param.23) | copy-start | bytes 3076
  24.8 4.9 %copy-start.4 = (bf16[256,4]{0,1:T(4,128)(2,1)S(1)}, bf16[256,4]{0,1:T(4,128)(2,1)}, u32[]{:S(2)}) copy-start(bf16[256,4]{0,1:T(4,128)(2,1)} %param.26) | copy-start | bytes 6148
  24.8 4.9 %copy-start.9 = (f32[4]{0:T(128)S(1)}, f32[4]{0:T(128)}, u32[]{:S(2)}) copy-start(f32[4]{0:T(128)} %param.27) | copy-start | bytes 52
  29.8 26.9 %copy-start.3 = (bf16[256,91]{0,1:T(8,128)(2,1)S(1)}, bf16[256,91]{0,1:T(8,128)(2,1)}, u32[]{:S(2)}) copy-start(bf16[256,91]{0,1:T(8,128)(2,1)} %param.20) | copy-start | bytes 139780
  29.8 27.0 %copy-start.5 = (f32[91]{0:T(128)S(1)}, f32[91]{0:T(128)}, u32[]{:S(2)}) copy-start(f32[91]{0:T(128)} %param.21) | copy-start | bytes 1096
  32.3 28.0 %copy-start.2 = (f32[2,4,2560]{2,1,0:T(4,128)}, f32[2,4,2560]{2,1,0:T(4,128)S(1)}, u32[]{:S(2)}) copy-start(f32[2,4,2560]{2,1,0:T(4,128)S(1)} %fusion.11) | copy-start | bytes 245764
  48.1 37.4 %all-to-all-start.2 = ((bf16[2,80,4]{2,0,1:T(2,128)(2,1)}), bf16[2,80,4]{2,0,1:T(2,128)(2,1)S(1)}, u32[]{:S(2)}, u32[]{:S(2)}) async-start(bf16[2,80,4]{2,0,1:T(2,128)(2,1)} %copy.57), calls=%async_computation.2 | async-start | bytes 81920 | tf_op jit(solution)/shard_map/all_to_all | solution.py:105
  85.5 10.8 %all-to-all-start.1 = ((bf16[2,80,91]{2,0,1:T(2,128)(2,1)}), bf16[2,80,91]{2,0,1:T(2,128)(2,1)S(1)}, u32[]{:S(2)}, u32[]{:S(2)}) async-start(bf16[2,80,91]{2,0,1:T(2,128)(2,1)} %copy.51), calls=%async_computation.1 | async-start | bytes 81920 | tf_op jit(solution)/shard_map/all_to_all | solution.py:104
  96.3 9.1 %all-to-all-start = ((bf16[2,80,256]{2,0,1:T(2,128)(2,1)}), bf16[2,80,256]{2,0,1:T(2,128)(2,1)S(1)}, u32[]{:S(2)}, u32[]{:S(2)}) async-start(bf16[2,80,256]{2,0,1:T(2,128)(2,1)} %copy.48), calls=%async_computation | async-start | bytes 163840 | tf_op jit(solution)/shard_map/all_to_all | solution.py:103
where the time goes:
time: 107 us; the launch traced here: 106 us
  blocking collectives  37.5 us (35%)
  local copies, waits for them, and re-layouts  23.6 us (22%)
  matrix products  13.5 us (13%)
  starting transfers between devices  13.3 us (12%)
  other arithmetic  11.1 us (10%)
  waiting for transfers between devices  6.06 us (6%)
    all_gather x1, blocking collectives, shards(): full_counts = lax.all_gather(counts, ('sy', 'sx'), axis=1, tiled=True)  10.3 us
    all_gather x1, blocking collectives, shards(): lax.all_gather(sel_feat, ('sy', 'sx'), axis=1, tiled=True)  9.54 us
    all_gather x1, blocking collectives, shards(): lax.all_gather(sel_boxes, ('sy', 'sx'), axis=1, tiled=True)  9.23 us
    all_gather x1, blocking collectives, shards(): lax.all_gather(sel_logits, ('sy', 'sx'), axis=1, tiled=True)  8.5 us
    convert_element_type x1, other arithmetic, shards(): (centered * lax.rsqrt(var + 1e-05) * norm_gain + norm_bias).astype(jnp.bf...  6.06 us
    all_to_all x1, starting transfers between devices, shards(): lax.all_to_all(gathered[1], 'img', split_axis=1, concat_axis=0, tiled=True)  5.13 us
    dot_general x1, matrix products, shards(): jnp.dot(hidden, box_w2, preferred_element_type=jnp.float32) + box_b2  4.9 us
    all_to_all x1, starting transfers between devices, shards(): lax.all_to_all(gathered[2], 'img', split_axis=1, concat_axis=0, tiled=True)  4.86 us
  transfers between devices with their start and end apart: 3, of which 2 were waited for; matrix products, arithmetic and copies ran while one was open for 19% of the time, Pallas kernels for 0%

commit v1 on v0

v1 whole, which is shorter than its diff:
```python
import functools
import jax
import jax.numpy as jnp
from jax import lax
from jax.experimental import pallas as pl
from jax.experimental.pallas import tpu as pltpu
from jax.sharding import PartitionSpec as P

TILE_H = 40
TILE_W = 64
Q_DEV = 20
MESH = pl.DeviceIdType.MESH
F32 = jnp.float32
BF = jnp.bfloat16


def up(n, m):
    return (n + m - 1) // m * m


def dot(a, b):
    return jnp.dot(a, b, preferred_element_type=F32)


def pad_lanes(x, lanes):
    if x.shape[1] == lanes:
        return x
    return jnp.concatenate([x, jnp.zeros((x.shape[0], lanes - x.shape[1]), x.dtype)], axis=1)


def transposed(ref):
    x = ref[...].astype(F32)
    return pad_lanes(x, up(x.shape[1], 128)).T.astype(BF)


def column(ref):
    x = pad_lanes(ref[...], up(ref.shape[1], 128))
    return jnp.broadcast_to(x, (128, x.shape[1])).T


def wide(col, lanes):
    return jnp.concatenate([col] * (lanes // 128), axis=1)


def prior_logit(center_x, center_y, k):
    prior = jnp.where(k == 0, center_x, jnp.where(k == 1, center_y, 0.05))
    return jnp.log(prior / (1.0 - prior))


def kernel(
    cfg,
    mem_hbm, we, be, ng, nb, wc, bc, w1, b1, w2, b2, w3, b3, picked, counts,
    logits_out, boxes_out, qf_out, ql_out, qb_out,
    mem_v, logits_v, boxes_v, wet, w1ct, w2t, w3t, bet, ngt, nbt, b1t, b2t, bct, b3t,
    sel, recv1, block, recv2,
    mem_sem, out_sem, send1, got1, send2, got2,
):
    n_img, n_sy, n_sx, chunk = cfg
    n = n_sy * n_sx
    images, tok, width = mem_v.shape
    cls = wc.shape[1]
    most = picked.shape[1]
    rows = sel.shape[1]
    g, sy, sx = lax.axis_index("img"), lax.axis_index("sy"), lax.axis_index("sx")
    tile = sy * n_sx + sx
    map_h, map_w = TILE_H * n_sy, TILE_W * n_sx
    my_i, my_q = tile // n_img, tile % n_img

    def at(img, t):
        return (img, t // n_sx, t % n_sx)

    loads = [pltpu.make_async_copy(mem_hbm.at[i], mem_v.at[i], mem_sem.at[i]) for i in range(images)]
    for load in loads:
        load.start()

    barrier = pltpu.get_barrier_semaphore()
    for off in range(1, n):
        pl.semaphore_signal(barrier, inc=1, device_id=at(g, (tile + off) % n), device_id_type=MESH)
    for off in range(1, n_img):
        for i in range(images):
            pl.semaphore_signal(
                barrier, inc=1, device_id=at((g + off) % n_img, i * n_img + g), device_id_type=MESH
            )

    wet[...] = transposed(we)
    w1ct[:width] = transposed(w1)
    w1ct[width:] = transposed(wc)[: w1ct.shape[0] - width]
    w2t[...] = transposed(w2)
    w3t[...] = transposed(w3)[: w3t.shape[0]]
    bet[...] = column(be)
    ngt[...] = column(ng)
    nbt[...] = column(nb)
    b1t[...] = column(b1)
    b2t[...] = column(b2)
    bct[...] = column(bc)
    b3t[...] = column(b3)[: b3t.shape[0]]

    diag = lax.broadcasted_iota(jnp.int32, (rows, most), 0) == lax.broadcasted_iota(jnp.int32, (rows, most), 1)
    spread = lax.broadcasted_iota(jnp.int32, (rows, tok), 1).astype(F32)
    real = lax.broadcasted_iota(jnp.int32, (rows, 1), 0) < most
    ids, mems = [], []
    for i in range(images):
        row = picked[i : i + 1, :].astype(F32)
        idx = jnp.sum(jnp.where(diag, row, 0.0), axis=1, keepdims=True)
        hot = jnp.where((spread == idx) & real, 1.0, 0.0).astype(BF)
        loads[i].wait()
        mems.append(dot(hot, mem_v[i]).astype(BF))
        ids.append(idx)
    mem_s = jnp.concatenate(mems, axis=0)
    idx = jnp.concatenate(ids, axis=0)
    pre = dot(mem_s, we[...]) + be[...]
    cen = pre - jnp.mean(pre, axis=1, keepdims=True)
    var = jnp.mean(cen * cen, axis=1, keepdims=True)
    out = (cen * lax.rsqrt(var + 1e-05) * ng[...] + nb[...]).astype(BF)
    cl = dot(out, pad_lanes(wc[...].astype(F32), 128).astype(BF)) + pad_lanes(bc[...], 128)
    hid = jnp.maximum(dot(out, w1[...]) + b1[...], 0.0).astype(BF)
    hid = jnp.maximum(dot(hid, w2[...]) + b2[...], 0.0).astype(BF)
    delta = dot(hid, pad_lanes(w3[...].astype(F32), 128).astype(BF)) + pad_lanes(b3[...], 128)
    at_row = jnp.floor((idx + 0.5) * (1.0 / TILE_W))
    at_col = idx - at_row * TILE_W
    cx = (at_col + (sx * TILE_W).astype(F32) + 0.5) / map_w
    cy = (at_row + (sy * TILE_H).astype(F32) + 0.5) / map_h
    lane = lax.broadcasted_iota(jnp.int32, delta.shape, 1)
    bx = pltpu.roll(jax.nn.sigmoid(delta + prior_logit(cx, cy, lane)), cls, 1)
    many = jnp.concatenate(
        [jnp.broadcast_to(counts[i : i + 1, :].astype(F32), (rows, 128)) for i in range(images)], axis=0
    )
    tail = jnp.where(lane < cls, cl, jnp.where(lane < cls + 4, bx, many)).astype(BF)
    for i in range(images):
        sel[i, :, :width] = out[i * rows : (i + 1) * rows]
        sel[i, :, width:] = tail[i * rows : (i + 1) * rows]

    pl.semaphore_wait(barrier, n - 1 + jnp.where(my_q == g, 0, n))

    sent = []
    for off in range(1, n):
        to = (tile + off) % n
        copy = pltpu.make_async_remote_copy(
            src_ref=sel.at[to // n_img], dst_ref=recv1.at[tile],
            send_sem=send1.at[off], recv_sem=got1.at[tile],
            device_id=at(g, to), device_id_type=MESH,
        )
        copy.start()
        sent.append(copy)
    own = pltpu.make_async_copy(sel.at[my_i], recv1.at[tile], got1.at[tile])
    own.start()

    def heads(i, first, count):
        def step(c, carry):
            lo = pl.multiple_of(c * chunk, 128)
            cols = pl.ds(lo, chunk)
            m = mem_v[i, cols, :]
            pre = lax.dot_general(wet[...], m, (((1,), (1,)), ((), ())), preferred_element_type=F32)
            pre = pre + wide(bet[...], chunk)
            cen = pre - jnp.mean(pre, axis=0, keepdims=True)
            var = jnp.mean(cen * cen, axis=0, keepdims=True)
            out = (cen * lax.rsqrt(var + 1e-05) * wide(ngt[...], chunk) + wide(nbt[...], chunk)).astype(BF)
            both = dot(w1ct[...], out)
            h = jnp.maximum(both[:width] + wide(b1t[...], chunk), 0.0).astype(BF)
            lg = both[width : width + cls] + wide(bct[:cls], chunk)
            logits_v[i, :, cols] = lg.astype(BF)
            h = jnp.maximum(dot(w2t[...], h) + wide(b2t[...], chunk), 0.0).astype(BF)
            delta = (dot(w3t[...], h) + wide(b3t[...], chunk))[:8]
            local = lo + lax.broadcasted_iota(jnp.int32, (8, chunk), 1)
            at_row = local // TILE_W
            at_col = local - at_row * TILE_W
            cx = ((at_col + sx * TILE_W).astype(F32) + 0.5) / map_w
            cy = ((at_row + sy * TILE_H).astype(F32) + 0.5) / map_h
            k = lax.broadcasted_iota(jnp.int32, (8, chunk), 0)
            boxes_v[i, :, cols] = jax.nn.sigmoid(delta + prior_logit(cx, cy, k))[:4]
            return carry

        lax.fori_loop(first, first + count, step, 0)

    outs = []

    def put(i):
        for a, b, s in ((logits_v, logits_out, 0), (boxes_v, boxes_out, 1)):
            copy = pltpu.make_async_copy(a.at[i], b.at[i], out_sem.at[i, s])
            copy.start()
            outs.append(copy)

    for i in range(images - 1):
        heads(i, 0, tok // chunk)
        put(i)

    own.wait()
    for off in range(1, n):
        frm = (tile + off) % n
        pltpu.make_async_remote_copy(
            src_ref=sel.at[0], dst_ref=recv1.at[frm], send_sem=send1.at[off], recv_sem=got1.at[frm],
            device_id=at(g, frm), device_id_type=MESH,
        ).wait_recv()
    start = (jnp.zeros((1, 1), F32) - (my_q * Q_DEV).astype(F32))
    k = lax.broadcasted_iota(jnp.int32, (rows, 128), 0).astype(F32)
    lane = lax.broadcasted_iota(jnp.int32, (rows, 128), 1).astype(F32)
    hots = []
    for s in range(n):
        have = recv1[s, :, width:].astype(F32)[0:1, cls + 4 : cls + 5]
        hots.append(jnp.where((k + start == lane) & (k < have), 1.0, 0.0))
        start = start + have
    hot = jnp.concatenate(hots, axis=0).T[: block.shape[0]].astype(BF)
    block[...] = dot(hot, recv1[...].reshape(n * rows, width + 128)).astype(BF)

    def hand(off):
        to = (tile + off) % n
        return pltpu.make_async_remote_copy(
            src_ref=block, dst_ref=recv2.at[g, my_i], send_sem=send2.at[off], recv_sem=got2.at[g, my_i],
            device_id=at(my_q, to), device_id_type=MESH,
        )

    for off in range(1, n):
        hand(off).start()

    @pl.when(my_q == g)
    def _():
        pltpu.make_async_copy(block, recv2.at[g, my_i], got2.at[g, my_i]).start()

    @pl.when(my_q != g)
    def _():
        hand(0).start()

    heads(images - 1, 0, tok // chunk)
    put(images - 1)

    for a in range(n_img):
        for i in range(images):
            pltpu.make_async_copy(block, recv2.at[a, i], got2.at[a, i]).wait()
            b = a * images + i
            qf_out[b] = recv2[a, i, :, :width][:Q_DEV]
            t = recv2[a, i, :, width:]
            ql_out[b] = t[:Q_DEV, :cls]
            qb_out[b] = pltpu.roll(t.astype(F32), 128 - cls, 1)[:Q_DEV, :4].astype(BF)

    for copy in sent:
        copy.wait_send()
    for off in range(1, n):
        hand(off).wait_send()

    @pl.when(my_q != g)
    def _():
        hand(0).wait_send()

    for copy in outs:
        copy.wait()


def shards(cfg, memory, we, be, ng, nb, wc, bc, w1, b1, w2, b2, w3, b3, picked, counts):
    n_img, n_sy, n_sx, chunk = cfg
    n = n_sy * n_sx
    images, tok, width = memory.shape
    cls = wc.shape[1]
    rows, qrows = up(picked.shape[1], 16), up(Q_DEV, 16)
    if images * n_img != n or cls + 5 > 128:
        raise ValueError("unsupported shape")
    total = images * n_img
    vm = pl.BlockSpec(memory_space=pltpu.VMEM)
    hbm = pl.BlockSpec(memory_space=pl.ANY)
    cpad = up(cls, 16)
    return pl.pallas_call(
        functools.partial(kernel, cfg),
        out_shape=(
            jax.ShapeDtypeStruct((images, cls, tok), BF),
            jax.ShapeDtypeStruct((images, 4, tok), F32),
            jax.ShapeDtypeStruct((total, Q_DEV, width), BF),
            jax.ShapeDtypeStruct((total, Q_DEV, cls), BF),
            jax.ShapeDtypeStruct((total, Q_DEV, 4), BF),
        ),
        in_specs=[hbm] + [vm] * 14,
        out_specs=(hbm, hbm, vm, vm, vm),
        scratch_shapes=[
            pltpu.VMEM((images, tok, width), BF),
            pltpu.VMEM((images, cls, tok), BF),
            pltpu.VMEM((images, 4, tok), F32),
            pltpu.VMEM((width, width), BF),
            pltpu.VMEM((width + cpad, width), BF),
            pltpu.VMEM((width, width), BF),
            pltpu.VMEM((16, width), BF),
            pltpu.VMEM((width, 128), F32),
            pltpu.VMEM((width, 128), F32),
            pltpu.VMEM((width, 128), F32),
            pltpu.VMEM((width, 128), F32),
            pltpu.VMEM((width, 128), F32),
            pltpu.VMEM((128, 128), F32),
            pltpu.VMEM((16, 128), F32),
            pltpu.VMEM((images, rows, width + 128), BF),
            pltpu.VMEM((n, rows, width + 128), BF),
            pltpu.VMEM((qrows, width + 128), BF),
            pltpu.VMEM((n_img, images, qrows, width + 128), BF),
            pltpu.SemaphoreType.DMA((images,)),
            pltpu.SemaphoreType.DMA((images, 2)),
            pltpu.SemaphoreType.DMA((n,)),
            pltpu.SemaphoreType.DMA((n,)),
            pltpu.SemaphoreType.DMA((n,)),
            pltpu.SemaphoreType.DMA((n_img, images)),
        ],
        compiler_params=pltpu.CompilerParams(collective_id=0, has_side_effects=True),
    )(
        memory, we, be[None], ng[None], nb[None], wc, bc[None], w1, b1[None], w2, b2[None], w3, b3[None],
        picked, counts,
    )


def solution(mesh):
    cfg = (mesh.shape["img"], mesh.shape["sy"], mesh.shape["sx"], 512)
    return jax.shard_map(
        functools.partial(shards, cfg),
        mesh=mesh,
        in_specs=(P("img", ("sy", "sx"), None),) + (P(),) * 12 + (P("img", ("sy", "sx")),) * 2,
        out_specs=(
            P("img", None, ("sy", "sx")),
            P("img", None, ("sy", "sx")),
            P(None, "img", None),
            P(None, "img", None),
            P(None, "img", None),
        ),
        check_vma=False,
    )
```

time: 107 us -> 39 us (0.36)
  blocking collectives: 37.5 us -> 0 us
  Pallas kernels: 0 us -> 24.5 us
  matrix products: 13.5 us -> 0 us
  starting transfers between devices: 13.3 us -> 0 us
  other arithmetic: 11.1 us -> 0 us
  local copies, waits for them, and re-layouts: 23.6 us -> 13.4 us
  waiting for transfers between devices: 6.06 us -> 0 us
    all_gather x4 -> x0, blocking collectives: 37.5 us -> none  [the longest x1 10.3 us: shards(): full_counts = lax.all_gather(counts, ('sy', 'sx'), axis=1, tiled=True)]
    pallas_call x0 -> x1, Pallas kernels: none -> 24.5 us  [shards(): pl.pallas_call(functools.partial(kernel, cfg), out_shape=(jax.ShapeDtypeS...]
    dot_general x7 -> x0, matrix products: 13.5 us -> none  [the longest x1 4.9 us: shards(): jnp.dot(hidden, box_w2, preferred_element_type=jnp.float32) + box_b2]
    all_to_all x3 -> x0, starting transfers between devices: 13.3 us -> none  [the longest x1 5.13 us: shards(): lax.all_to_all(gathered[1], 'img', split_axis=1, concat_axis=0, tiled=True)]
    gather x5 -> x0, local copies, waits for them, and re-layouts: 11.3 us -> none  [the longest x2 3.85 us: shards(): jnp.take_along_axis(token_boxes, picked[:, None, :], axis=2)]
    pallas_call x0 -> x4, local copies, waits for them, and re-layouts: none -> 7.58 us  [shards(): pl.pallas_call(functools.partial(kernel, cfg), out_shape=(jax.ShapeDtypeS...]
    convert_element_type x2 -> x0, other arithmetic: 6.07 us -> none  [the longest x1 6.06 us: shards(): (centered * lax.rsqrt(var + 1e-05) * norm_gain + norm_bias).astype(jnp.bf...]
    all_to_all x3 -> x0, waiting for transfers between devices: 6.06 us -> none  [the longest x1 4.77 us: shards(): lax.all_to_all(gathered[1], 'img', split_axis=1, concat_axis=0, tiled=True)]
  transfers between devices with their start and end apart: 3 -> 0, of which waited for: 2 -> 0; matrix products, arithmetic and copies ran while one was open for 19% -> 0% of each run, Pallas kernels for 0% -> 0%
where the time goes in v1:
time: 39 us; the launch traced here: 38.5 us
  Pallas kernels  24.5 us (63%)
  local copies, waits for them, and re-layouts  13.4 us (34%)
  between operations  0.64 us (2%)
    pallas_call x1, Pallas kernels, shards(): pl.pallas_call(functools.partial(kernel, cfg), out_shape=(jax.ShapeDtypeS...  24.5 us
    pallas_call x4, local copies, waits for them, and re-layouts, shards(): pl.pallas_call(functools.partial(kernel, cfg), out_shape=(jax.ShapeDtypeS...  7.58 us
    unnamed x4, local copies, waits for them, and re-layouts  5.79 us

profile of v1, /device:TPU:0, one launch (start us, length us, event | category | flops | bytes accessed | tf_op | source)
XLA Modules:
  0.0 38.5 jit_solution(12427777266348055524)
XLA Ops:
  0.6 1.3 %copy.22.counts = s32[2,1]{1,0:T(2,128)} copy(s32[2,1]{0,1:T(1,128)} %param.29) | data formatting | bytes 16 | tf_op args[14]
  1.9 1.5 %copy.20.wc = bf16[256,91]{1,0:T(8,128)(2,1)} copy(bf16[256,91]{0,1:T(8,128)(2,1)} %param.20) | data formatting | bytes 93184 | tf_op args[5]
  3.5 1.4 %copy.21.w3 = bf16[256,4]{1,0:T(8,128)(2,1)} copy(bf16[256,4]{0,1:T(4,128)(2,1)} %param.26) | data formatting | bytes 4096 | tf_op args[11]
  4.9 24.5 %shard_map.182 = (bf16[2,91,2560]{2,1,0:T(8,128)(2,1)}, f32[2,4,2560]{2,1,0:T(4,128)}, bf16[8,20,256]{2,1,0:T(8,128)(2,1)}, bf16[8,20,91]{2,1,0:T(8,128)(2,1)}, bf16[8,20,4]{2,1,0:T(8,128)(2,1)}) custom-call(bf16[2,2560,256]{2,1,0:T(8,128)(2,1)} %mem_hbm.1, bf16[256,256]{1,0:T(8,128)(2,1)} %we.1, f32[1,256]{1,0:T(1,128)} %bitcast.7, f32[1,256]{1,0:T(1,128)} %bitcast.8, ...), custom_call_target="tpu_custom_call" | custom-call | tf_op jit(solution)/shard_map/pallas_call | solution.py:260
  29.4 3.1 %copy.23 = bf16[2,91,2560]{2,0,1:T(2,128)(2,1)} copy(bf16[2,91,2560]{2,1,0:T(8,128)(2,1)} %get-tuple-element.5) | data formatting | bytes 1863680 | tf_op jit(solution)/shard_map/pallas_call | solution.py:260
  32.5 1.5 %copy.26 = bf16[8,20,4]{1,2,0:T(4,128)(2,1)} copy(bf16[8,20,4]{2,1,0:T(8,128)(2,1)} %get-tuple-element.9) | data formatting | bytes 2560 | tf_op jit(solution)/shard_map/pallas_call | solution.py:260
  34.1 1.4 %copy.25 = bf16[8,20,91]{2,0,1:T(8,128)(2,1)} copy(bf16[8,20,91]{2,1,0:T(8,128)(2,1)} %get-tuple-element.8) | data formatting | bytes 58240 | tf_op jit(solution)/shard_map/pallas_call | solution.py:260
  35.5 1.5 %copy.24 = bf16[8,20,256]{2,0,1:T(8,128)(2,1)} copy(bf16[8,20,256]{2,1,0:T(8,128)(2,1)} %get-tuple-element.7) | data formatting | bytes 163840 | tf_op jit(solution)/shard_map/pallas_call | solution.py:260
  37.0 1.5 %copy.28 = f32[2,4,2560]{2,1,0:T(4,128)} copy(f32[2,4,2560]{2,1,0:T(4,128)} %get-tuple-element.16) | data formatting | bytes 163840

commit v2 on v1

v2 whole, which is shorter than its diff:
```python
import functools
import jax
import jax.numpy as jnp
from jax import lax
from jax.experimental import pallas as pl
from jax.experimental.pallas import tpu as pltpu
from jax.sharding import PartitionSpec as P

TILE_H = 40
TILE_W = 64
Q_DEV = 20
MESH = pl.DeviceIdType.MESH
F32 = jnp.float32
BF = jnp.bfloat16


def up(n, m):
    return (n + m - 1) // m * m


def dot(a, b):
    return jnp.dot(a, b, preferred_element_type=F32)


def dot_nt(a, b):
    return lax.dot_general(a, b, (((1,), (1,)), ((), ())), preferred_element_type=F32)


def pad_lanes(x, lanes):
    if x.shape[1] == lanes:
        return x
    return jnp.concatenate([x, jnp.zeros((x.shape[0], lanes - x.shape[1]), x.dtype)], axis=1)


def transposed(ref):
    x = ref[...].astype(F32)
    return pad_lanes(x, up(x.shape[1], 128)).T.astype(BF)


def column(ref):
    x = pad_lanes(ref[...], up(ref.shape[1], 128))
    return jnp.broadcast_to(x, (128, x.shape[1])).T


def pad_rows(x, rows):
    if x.shape[0] == rows:
        return x
    return jnp.concatenate([x, jnp.zeros((rows - x.shape[0], x.shape[1]), x.dtype)], axis=0)


def prepare(we, be, ng, nb, wct, bc, w1, b1, w2, b2, w3t, b3, images, prep):
    p_we, p_wc, p_w1, p_w2, p_w3, p_be, p_ng, p_nb, p_b1, p_b2, p_bc, p_b3 = prep
    cls, width = wct.shape
    p_we[...] = transposed(we)
    p_w1[...] = transposed(w1)
    p_w2[...] = transposed(w2)
    p_w3[...] = pad_rows(w3t[...].astype(F32), 16).astype(BF)
    xr = p_wc.shape[0]
    r = lax.broadcasted_iota(jnp.int32, (xr, 128), 0)
    c = lax.broadcasted_iota(jnp.int32, (xr, 128), 1)
    wpad = pad_rows(wct[...].astype(F32), 128).astype(BF)
    for i in range(images):
        pick = jnp.where(r == c * images + i, 1.0, 0.0).astype(BF)
        p_wc[:, i * width : (i + 1) * width] = dot(pick, wpad).astype(BF)
    mine = (r >= c * images) & (r < (c + 1) * images)
    p_bc[...] = jnp.broadcast_to(
        jnp.sum(jnp.where(mine, pad_lanes(bc[...], 128), 0.0), axis=1, keepdims=True), (xr, 128)
    )
    for p, v in ((p_be, be), (p_ng, ng), (p_nb, nb), (p_b1, b1), (p_b2, b2)):
        p[...] = column(v)
    p_b3[...] = column(b3)[: p_b3.shape[0]]


def prep_shapes(images, cls, width):
    xr = up(images * cls, 16)
    return [
        pltpu.VMEM((width, width), BF),
        pltpu.VMEM((xr, images * width), BF),
        pltpu.VMEM((width, width), BF),
        pltpu.VMEM((width, width), BF),
        pltpu.VMEM((16, width), BF),
    ] + [pltpu.VMEM((width, 128), F32)] * 5 + [pltpu.VMEM((xr, 128), F32), pltpu.VMEM((16, 128), F32)]


def heads(prep, mem_v, logits_v, boxes_v, lo, at_lo, chunk, place):
    p_we, p_wc, p_w1, p_w2, p_w3, p_be, p_ng, p_nb, p_b1, p_b2, p_bc, p_b3 = prep
    images, cls = mem_v.shape[0], logits_v.shape[0]
    sy, sx, map_h, map_w, first = place
    cols = pl.ds(at_lo, chunk)
    local = first + lo + lax.broadcasted_iota(jnp.int32, (8, chunk), 1)
    at_row = local // TILE_W
    at_col = local - at_row * TILE_W
    cx = ((at_col + sx * TILE_W).astype(F32) + 0.5) / map_w
    cy = ((at_row + sy * TILE_H).astype(F32) + 0.5) / map_h
    prior = prior_logit(cx, cy, lax.broadcasted_iota(jnp.int32, (8, chunk), 0))
    out_all = []
    for i in range(images):
        m = mem_v[i, pl.ds(lo, chunk), :]
        pre = lax.dot_general(p_we[...], m, (((1,), (1,)), ((), ())), preferred_element_type=F32)
        pre = pre + wide(p_be[...], chunk)
        cen = pre - jnp.mean(pre, axis=0, keepdims=True)
        var = jnp.mean(cen * cen, axis=0, keepdims=True)
        out = (cen * lax.rsqrt(var + 1e-05) * wide(p_ng[...], chunk) + wide(p_nb[...], chunk)).astype(BF)
        out_all.append(out)
        h = jnp.maximum(dot(p_w1[...], out) + wide(p_b1[...], chunk), 0.0).astype(BF)
        h = jnp.maximum(dot(p_w2[...], h) + wide(p_b2[...], chunk), 0.0).astype(BF)
        delta = (dot(p_w3[...], h) + wide(p_b3[...], chunk))[:8]
        boxes_v[i, :, cols] = jax.nn.sigmoid(delta + prior)[:4]
    lg = dot(p_wc[...], jnp.concatenate(out_all, axis=0)) + wide(p_bc[...], chunk)
    logits_v[:, :, cols] = lg.astype(BF)[: cls * images].reshape(cls, images, chunk)


def wide(col, lanes):
    return jnp.concatenate([col] * (lanes // 128), axis=1)


def prior_logit(center_x, center_y, k):
    prior = jnp.where(k == 0, center_x, jnp.where(k == 1, center_y, 0.05))
    return jnp.log(prior / (1.0 - prior))


def kernel(
    cfg,
    mem_hbm, we, be, ng, nb, wct, bc, w1, b1, w2, b2, w3t, b3, picked, counts,
    logits_v, boxes_v, qf_out, ql_out, qb_out,
    mem_v, sel, recv1, block, recv2, mem_sem, send1, got1, send2, got2,
    *prep,
):
    n_img, n_sy, n_sx, chunk, early, late = cfg
    n = n_sy * n_sx
    images, tok, width = mem_v.shape
    cls = wct.shape[0]
    most = picked.shape[1]
    rows = sel.shape[1]
    g, sy, sx = lax.axis_index("img"), lax.axis_index("sy"), lax.axis_index("sx")
    tile = sy * n_sx + sx
    map_h, map_w = TILE_H * n_sy, TILE_W * n_sx
    my_i, my_q = tile // n_img, tile % n_img

    def at(img, t):
        return (img, t // n_sx, t % n_sx)

    loads = [pltpu.make_async_copy(mem_hbm.at[i], mem_v.at[i], mem_sem.at[i]) for i in range(images)]
    for load in loads:
        load.start()

    barrier = pltpu.get_barrier_semaphore()
    for off in range(1, n):
        pl.semaphore_signal(barrier, inc=1, device_id=at(g, (tile + off) % n), device_id_type=MESH)
    for off in range(1, n_img):
        for i in range(images):
            pl.semaphore_signal(
                barrier, inc=1, device_id=at((g + off) % n_img, i * n_img + g), device_id_type=MESH
            )

    prepare(we, be, ng, nb, wct, bc, w1, b1, w2, b2, w3t, b3, images, prep)
    place = (sy, sx, map_h, map_w, 0)

    diag = lax.broadcasted_iota(jnp.int32, (rows, most), 0) == lax.broadcasted_iota(jnp.int32, (rows, most), 1)
    spread = lax.broadcasted_iota(jnp.int32, (rows, tok), 1).astype(F32)
    real = lax.broadcasted_iota(jnp.int32, (rows, 1), 0) < most
    ids, mems = [], []
    for i in range(images):
        row = picked[i : i + 1, :].astype(F32)
        idx = jnp.sum(jnp.where(diag, row, 0.0), axis=1, keepdims=True)
        hot = jnp.where((spread == idx) & real, 1.0, 0.0).astype(BF)
        loads[i].wait()
        mems.append(dot(hot, mem_v[i]).astype(BF))
        ids.append(idx)
    mem_s = jnp.concatenate(mems, axis=0)
    idx = jnp.concatenate(ids, axis=0)
    pre = dot(mem_s, we[...]) + be[...]
    cen = pre - jnp.mean(pre, axis=1, keepdims=True)
    var = jnp.mean(cen * cen, axis=1, keepdims=True)
    out = (cen * lax.rsqrt(var + 1e-05) * ng[...] + nb[...]).astype(BF)
    wpad = pad_rows(wct[...].astype(F32), 128).astype(BF)
    cl = dot_nt(out, wpad) + pad_lanes(bc[...], 128)
    hid = jnp.maximum(dot(out, w1[...]) + b1[...], 0.0).astype(BF)
    hid = jnp.maximum(dot(hid, w2[...]) + b2[...], 0.0).astype(BF)
    delta = dot_nt(hid, pad_rows(w3t[...].astype(F32), 128).astype(BF)) + pad_lanes(b3[...], 128)
    at_row = jnp.floor((idx + 0.5) * (1.0 / TILE_W))
    at_col = idx - at_row * TILE_W
    cx = (at_col + (sx * TILE_W).astype(F32) + 0.5) / map_w
    cy = (at_row + (sy * TILE_H).astype(F32) + 0.5) / map_h
    lane = lax.broadcasted_iota(jnp.int32, delta.shape, 1)
    bx = pltpu.roll(jax.nn.sigmoid(delta + prior_logit(cx, cy, lane)), cls, 1)
    many = jnp.concatenate(
        [jnp.broadcast_to(counts[:, i : i + 1].astype(F32), (rows, 128)) for i in range(images)], axis=0
    )
    tail = jnp.where(lane < cls, cl, jnp.where(lane < cls + 4, bx, many)).astype(BF)
    for i in range(images):
        sel[i, :, :width] = out[i * rows : (i + 1) * rows]
        sel[i, :, width:] = tail[i * rows : (i + 1) * rows]

    pl.semaphore_wait(barrier, n - 1 + jnp.where(my_q == g, 0, n))

    sent = []
    for off in range(1, n):
        to = (tile + off) % n
        copy = pltpu.make_async_remote_copy(
            src_ref=sel.at[to // n_img], dst_ref=recv1.at[tile],
            send_sem=send1.at[off], recv_sem=got1.at[tile],
            device_id=at(g, to), device_id_type=MESH,
        )
        copy.start()
        sent.append(copy)
    own = pltpu.make_async_copy(sel.at[my_i], recv1.at[tile], got1.at[tile])
    own.start()

    def some(first, count):
        def step(c, carry):
            lo = pl.multiple_of(c * chunk, 128)
            heads(prep, mem_v, logits_v, boxes_v, lo, lo, chunk, place)
            return carry

        lax.fori_loop(first, first + count, step, 0)

    some(0, early)

    own.wait()
    for off in range(1, n):
        frm = (tile + off) % n
        pltpu.make_async_remote_copy(
            src_ref=sel.at[0], dst_ref=recv1.at[frm], send_sem=send1.at[off], recv_sem=got1.at[frm],
            device_id=at(g, frm), device_id_type=MESH,
        ).wait_recv()
    start = (jnp.zeros((1, 1), F32) - (my_q * Q_DEV).astype(F32))
    k = lax.broadcasted_iota(jnp.int32, (rows, 128), 0).astype(F32)
    lane = lax.broadcasted_iota(jnp.int32, (rows, 128), 1).astype(F32)
    hots = []
    for s in range(n):
        have = recv1[s, :, width:].astype(F32)[0:1, cls + 4 : cls + 5]
        hots.append(jnp.where((k + start == lane) & (k < have), 1.0, 0.0))
        start = start + have
    hot = jnp.concatenate(hots, axis=0).T[: block.shape[0]].astype(BF)
    block[...] = dot(hot, recv1[...].reshape(n * rows, width + 128)).astype(BF)

    def hand(off):
        to = (tile + off) % n
        return pltpu.make_async_remote_copy(
            src_ref=block, dst_ref=recv2.at[g, my_i], send_sem=send2.at[off], recv_sem=got2.at[g, my_i],
            device_id=at(my_q, to), device_id_type=MESH,
        )

    for off in range(1, n):
        hand(off).start()

    @pl.when(my_q == g)
    def _():
        pltpu.make_async_copy(block, recv2.at[g, my_i], got2.at[g, my_i]).start()

    @pl.when(my_q != g)
    def _():
        hand(0).start()

    some(early, late)

    for a in range(n_img):
        for i in range(images):
            pltpu.make_async_copy(block, recv2.at[a, i], got2.at[a, i]).wait()
    total, qrows = n_img * images, block.shape[0]
    every = recv2[...].reshape(total * qrows, width + 128)
    r = lax.broadcasted_iota(jnp.int32, (Q_DEV * total, total * qrows), 0)
    c = lax.broadcasted_iota(jnp.int32, (Q_DEV * total, total * qrows), 1)
    turn = jnp.where(r % total * qrows + r // total == c, 1.0, 0.0).astype(BF)
    done = dot(turn, every).reshape(Q_DEV, total, width + 128)
    qf_out[...] = done[:, :, :width].astype(BF)
    ql_out[...] = done[:, :, width : width + cls].astype(BF)
    lane = lax.broadcasted_iota(jnp.int32, (16, 128), 1)
    k = lax.broadcasted_iota(jnp.int32, (16, 128), 0)
    which = jnp.where(lane == k + cls, 1.0, 0.0).astype(BF)
    for b in range(total):
        qb_out[b] = dot_nt(which, recv2[b // images, b % images, :, width:])[:4, :Q_DEV].astype(BF)

    for copy in sent:
        copy.wait_send()
    for off in range(1, n):
        hand(off).wait_send()

    @pl.when(my_q != g)
    def _():
        hand(0).wait_send()


def finish(
    cfg,
    mem_hbm, we, be, ng, nb, wct, bc, w1, b1, w2, b2, w3t, b3, logits_a, boxes_a, qf, ql, qb,
    logits_out, boxes_out, qf_out, ql_out, qb_out,
    mem_v, logits_v, boxes_v, mem_sem, out_sem,
    *prep,
):
    n_img, n_sy, n_sx, chunk, early, late = cfg
    images, rest, width = mem_v.shape
    done = (early + late) * chunk
    sy, sx = lax.axis_index("sy"), lax.axis_index("sx")
    load = pltpu.make_async_copy(mem_hbm.at[:, pl.ds(done, rest), :], mem_v, mem_sem)
    load.start()
    outs = [
        pltpu.make_async_copy(logits_a, logits_out.at[:, :, pl.ds(0, done)], out_sem.at[0]),
        pltpu.make_async_copy(boxes_a, boxes_out.at[:, :, pl.ds(0, done)], out_sem.at[1]),
    ]
    for copy in outs:
        copy.start()
    prepare(we, be, ng, nb, wct, bc, w1, b1, w2, b2, w3t, b3, images, prep)
    qf_out[...] = qf[...]
    ql_out[...] = ql[...]
    qb_out[...] = qb[...]
    load.wait()
    place = (sy, sx, TILE_H * n_sy, TILE_W * n_sx, done)

    def step(c, carry):
        lo = pl.multiple_of(c * chunk, 128)
        heads(prep, mem_v, logits_v, boxes_v, lo, lo, chunk, place)
        return carry

    lax.fori_loop(0, rest // chunk, step, 0)
    last = [
        pltpu.make_async_copy(logits_v, logits_out.at[:, :, pl.ds(done, rest)], out_sem.at[2]),
        pltpu.make_async_copy(boxes_v, boxes_out.at[:, :, pl.ds(done, rest)], out_sem.at[3]),
    ]
    for copy in last:
        copy.start()
    for copy in outs + last:
        copy.wait()


def shards(cfg, memory, we, be, ng, nb, wc, bc, w1, b1, w2, b2, w3, b3, picked, counts):
    n_img, n_sy, n_sx, chunk, early, late = cfg
    n = n_sy * n_sx
    images, tok, width = memory.shape
    cls = wc.shape[1]
    rows, qrows = up(picked.shape[1], 16), up(Q_DEV, 16)
    if images * n_img != n or cls + 5 > 128 or tok % chunk:
        raise ValueError("unsupported shape")
    total = images * n_img
    done = (early + late) * chunk
    vm = pl.BlockSpec(memory_space=pltpu.VMEM)
    hbm = pl.BlockSpec(memory_space=pl.ANY)
    weights = (we, be[None], ng[None], nb[None], wc.T, bc[None], w1, b1[None], w2, b2[None], w3.T, b3[None])

    def dense(count):
        return (jax.ShapeDtypeStruct((cls, images, count), BF), jax.ShapeDtypeStruct((images, 4, count), F32))

    slots = (
        jax.ShapeDtypeStruct((Q_DEV, total, width), BF),
        jax.ShapeDtypeStruct((Q_DEV, total, cls), BF),
        jax.ShapeDtypeStruct((total, 4, Q_DEV), BF),
    )
    first = pl.pallas_call(
        functools.partial(kernel, cfg),
        out_shape=dense(done) + slots,
        in_specs=[hbm] + [vm] * 14,
        out_specs=(vm,) * 5,
        scratch_shapes=[
            pltpu.VMEM((images, tok, width), BF),
            pltpu.VMEM((images, rows, width + 128), BF),
            pltpu.VMEM((n, rows, width + 128), BF),
            pltpu.VMEM((qrows, width + 128), BF),
            pltpu.VMEM((n_img, images, qrows, width + 128), BF),
            pltpu.SemaphoreType.DMA((images,)),
            pltpu.SemaphoreType.DMA((n,)),
            pltpu.SemaphoreType.DMA((n,)),
            pltpu.SemaphoreType.DMA((n,)),
            pltpu.SemaphoreType.DMA((n_img, images)),
        ] + prep_shapes(images, cls, width),
        compiler_params=pltpu.CompilerParams(collective_id=0, has_side_effects=True),
        name="exchange",
    )(memory, *weights, picked, counts.T)
    rest = tok - done
    logits, boxes, qf, ql, qb = pl.pallas_call(
        functools.partial(finish, cfg),
        out_shape=dense(tok) + slots,
        in_specs=[hbm] + [vm] * 17,
        out_specs=(hbm, hbm, vm, vm, vm),
        scratch_shapes=[
            pltpu.VMEM((images, rest, width), BF),
            pltpu.VMEM((cls, images, rest), BF),
            pltpu.VMEM((images, 4, rest), F32),
            pltpu.SemaphoreType.DMA,
            pltpu.SemaphoreType.DMA((4,)),
        ] + prep_shapes(images, cls, width),
        name="finish",
    )(memory, *weights, *first)
    return (
        jnp.transpose(logits, (1, 0, 2)), boxes, jnp.transpose(qf, (1, 0, 2)), jnp.transpose(ql, (1, 0, 2)),
        jnp.transpose(qb, (0, 2, 1)),
    )


def solution(mesh):
    cfg = (mesh.shape["img"], mesh.shape["sy"], mesh.shape["sx"], 256, 2, 3)
    return jax.shard_map(
        functools.partial(shards, cfg),
        mesh=mesh,
        in_specs=(P("img", ("sy", "sx"), None),) + (P(),) * 12 + (P("img", ("sy", "sx")),) * 2,
        out_specs=(
            P("img", None, ("sy", "sx")),
            P("img", None, ("sy", "sx")),
            P(None, "img", None),
            P(None, "img", None),
            P(None, "img", None),
        ),
        check_vma=False,
    )
```

time: 39 us -> 37.4 us (0.959)
  local copies, waits for them, and re-layouts: 13.4 us -> 0 us
  Pallas kernels: 24.5 us -> 36.6 us
    pallas_call x1 -> x2, Pallas kernels: 24.5 us -> 36.6 us  [the longest x1 24.6 us: shards(): pl.pallas_call(functools.partial(kernel, cfg), out_shape=dense(done) + sl...]
    pallas_call x4 -> x0, local copies, waits for them, and re-layouts: 7.58 us -> none  [shards(): pl.pallas_call(functools.partial(kernel, cfg), out_shape=(jax.ShapeDtypeS...]
    unnamed x4 -> x0, local copies, waits for them, and re-layouts: 5.79 us -> none
where the time goes in v2:
time: 37.4 us; the launch traced here: 37.2 us
  Pallas kernels  36.6 us (98%)
  between operations  0.64 us (2%)
    pallas_call x1, Pallas kernels, shards(): pl.pallas_call(functools.partial(kernel, cfg), out_shape=dense(done) + sl...  24.6 us
    pallas_call x1, Pallas kernels, shards(): pl.pallas_call(functools.partial(finish, cfg), out_shape=dense(tok) + slo...  12 us

profile of v2, /device:TPU:0, one launch (start us, length us, event | category | flops | bytes accessed | tf_op | source)
XLA Modules:
  0.0 37.2 jit_solution(778500159406826994)
XLA Ops:
  0.6 24.6 %exchange.1 = (bf16[91,2,1280]{2,1,0:T(2,128)(2,1)}, f32[2,4,1280]{2,1,0:T(4,128)}, bf16[20,8,256]{2,1,0:T(8,128)(2,1)}, bf16[20,8,91]{2,1,0:T(8,128)(2,1)}, bf16[8,4,20]{2,1,0:T(4,128)(2,1)}) custom-call(bf16[2,2560,256]{2,1,0:T(8,128)(2,1)} %mem_hbm.3, bf16[256,256]{1,0:T(8,128)(2,1)} %we.3, f32[1,256]{1,0:T(1,128)} %bitcast.18, f32[1,256]{1,0:T(1,128)} %bitcast.20, ...), custom_call_target="tpu_custom_call" | custom-call | tf_op jit(solution)/shard_map/exchange/pallas_call | solution.py:349
  25.2 12.0 %finish.1 = (bf16[91,2,2560]{2,1,0:T(2,128)(2,1)}, f32[2,4,2560]{2,1,0:T(4,128)}, bf16[20,8,256]{2,1,0:T(8,128)(2,1)}, bf16[20,8,91]{2,1,0:T(8,128)(2,1)}, bf16[8,4,20]{2,1,0:T(4,128)(2,1)}) custom-call(bf16[2,2560,256]{2,1,0:T(8,128)(2,1)} %mem_hbm.3, bf16[256,256]{1,0:T(8,128)(2,1)} %we.3, f32[1,256]{1,0:T(1,128)} %bitcast.19, f32[1,256]{1,0:T(1,128)} %bitcast.21, ...), custom_call_target="tpu_custom_call" | custom-call | tf_op jit(solution)/shard_map/finish/pallas_call | solution.py:370
